TPU v7x, 256 devices: a whole 4x4x8 slice. The times are simulated.
256 devices in a mesh: ty: 8 (over z_hi, y), tx: 32 (over z_lo, x, core).
Axes of the slice: x: 4, y: 4, z: 8 (z_hi: 2, z_lo: 4; z = z_hi * 4 + z_lo), core: 2. Of those that a mesh axis runs over, the one named last changes fastest.
Arguments:
- tracer_start: float32 [48, 128, 4096], P(None, 'ty', 'tx'), may hold values from -6 to 6
- observed: bfloat16 [48, 128, 4096], P(None, 'ty', 'tx'), may hold values from -6 to 6
- east_speed: bfloat16 [48, 128, 4096], P(None, 'ty', 'tx'), may hold values from -4 to 4
- north_speed: bfloat16 [48, 128, 4096], P(None, 'ty', 'tx'), may hold values from -4 to 4
- mixing: bfloat16 [48, 128, 4096], P(None, 'ty', 'tx'), may hold values from 0.019897461 to 0.19921875
- vertical_mixing: bfloat16 [47, 128, 4096], P(None, 'ty', 'tx'), may hold values from 0.19921875 to 5
- relax_rate: bfloat16 [48, 128, 4096], P(None, 'ty', 'tx'), may hold values from 0.049804688 to 0.5
- level_count: int32 [128, 4096], P('ty', 'tx'), may hold values from 0 to 48, as said below
- face_east: int32 [128, 4096], P('ty', 'tx'), may hold values from 0 to 48, as said below
- face_north: int32 [128, 4096], P('ty', 'tx'), may hold values from 0 to 48, as said below
Outputs:
- adjoint_start: float32 [48, 128, 4096], P(None, 'ty', 'tx')
- mixing_gradient: float32 [48, 128, 4096], P(None, 'ty', 'tx')
Inputs may be any that keep to these rules, and one draw needn't show every extreme that they name: Levels 0 to level_count - 1 of a column are water; 0 marks land. `face_east`: the smaller of the level counts of a column and of the next column east, the last column's next being the first. `face_north`: the smaller of the level counts of a column and of the next row's column north, the last row's next being the first.
All inputs are finite; a program needn't handle non-finite values.
Results may differ from a plain program's by a relative error of at most 0.0006.
Values sent between devices are 32-bit elements; how exact they have to be, the bound alone decides.
A program may use at most 64 MiB of HBM per device.

v0:
```python
import functools

import jax
import jax.numpy as jnp
from jax import lax
from jax.experimental import pallas as pl
from jax.experimental.pallas import tpu as pltpu
from jax.sharding import PartitionSpec as P

EAST, WEST, NORTH, SOUTH = range(4)
UNROLL = 4
CHAIN_UNROLL = 8


def kernel(
    sizes,
    tracer_hbm, observed_hbm, east_hbm, north_hbm, mixing_hbm, vertical_hbm, relax_hbm,
    count_hbm, face_east_hbm, face_north_hbm,
    adjoint_hbm, gradient_hbm,
    start, observed, east, north, mixing, vertical, relax, count, face_east, face_north,
    east_minus, east_plus, north_minus, north_plus, sink,
    inverse, ratio, feed,
    middle, rhs, carry, solved_two, solved_one, gradient,
    to_east0, to_north0, to_west0, to_south0,
    to_east, to_west, to_north, to_south,
    from_west0, from_south0, from_east0, from_north0,
    from_west, from_east, from_south, from_north,
    load_sem, store_sem, send_sem, recv_sem,
):
    levels, rows, lanes, size_y, size_x = sizes
    my_y = lax.axis_index("ty")
    my_x = lax.axis_index("tx")
    neighbour = {
        EAST: {"tx": lax.rem(my_x + 1, size_x)},
        WEST: {"tx": lax.rem(my_x + size_x - 1, size_x)},
        NORTH: {"ty": lax.rem(my_y + 1, size_y)},
        SOUTH: {"ty": lax.rem(my_y + size_y - 1, size_y)},
    }
    barrier = pltpu.get_barrier_semaphore()
    for side in range(4):
        pl.semaphore_signal(
            barrier, inc=1, device_id=neighbour[side], device_id_type=pl.DeviceIdType.MESH
        )

    loads = [
        pltpu.make_async_copy(source, target, load_sem.at[slot])
        for slot, (source, target) in enumerate(
            (
                (tracer_hbm, start),
                (east_hbm, east),
                (north_hbm, north),
                (mixing_hbm, mixing),
                (face_east_hbm, face_east),
                (face_north_hbm, face_north),
                (vertical_hbm, vertical),
                (count_hbm, count),
                (relax_hbm, relax),
                (observed_hbm, observed),
            )
        )
    ]
    for load in loads:
        load.start()
    for load in loads[:6]:
        load.wait()

    lane = lax.broadcasted_iota(jnp.int32, (rows, lanes), 1)
    row = lax.broadcasted_iota(jnp.int32, (rows, lanes), 0)
    first_lane, last_lane = lane == 0, lane == lanes - 1
    rim_lanes = first_lane | last_lane
    first_row, last_row = row == 0, row == rows - 1
    even_lane = lane % 2 == 0
    zero = jnp.zeros((rows, lanes), jnp.float32)

    def at(height):
        return pl.ds(pl.multiple_of(height * rows, rows), rows)

    def from_lane_east(block):
        return jnp.where(last_lane, 0.0, pltpu.roll(block, lanes - 1, 1))

    def from_lane_west(block):
        return jnp.where(first_lane, 0.0, pltpu.roll(block, 1, 1))

    def from_row_north(block):
        return jnp.where(last_row, 0.0, pltpu.roll(block, rows - 1, 0))

    def from_row_south(block):
        return jnp.where(first_row, 0.0, pltpu.roll(block, 1, 0))

    def pack(packed, block, height):
        turned = pltpu.roll(block, 2 * height, 1)
        mine = ((lane + 1) % lanes) // 2 == height
        return jnp.where(mine, turned, packed)

    def unpack(packed, height):
        return jnp.where(rim_lanes, pltpu.roll(packed, lax.rem(lanes - 2 * height, lanes), 1), 0.0)

    def south_row(ref):
        return ref[pl.ds(0, levels, stride=rows), :]

    def north_row(ref):
        return ref[pl.ds(rows - 1, levels, stride=rows), :]

    def add_rows(ref, south, north):
        low = pl.ds(0, levels, stride=rows)
        high = pl.ds(rows - 1, levels, stride=rows)
        ref[low, :] = ref[low, :] + south
        ref[high, :] = ref[high, :] + north

    def loop(body, init, unroll=UNROLL):
        return lax.fori_loop(0, levels, body, init, unroll=unroll)

    def remote(source, target, slot, side):
        return pltpu.make_async_remote_copy(
            src_ref=source,
            dst_ref=target,
            send_sem=send_sem.at[slot, side],
            recv_sem=recv_sem.at[slot, side],
            device_id=neighbour[side],
            device_id_type=pl.DeviceIdType.MESH,
        )

    open_to_east = face_east[...]
    open_to_north = face_north[...]

    def coefficients(height, packs):
        own = start[at(height), :]
        spread = mixing[height].astype(jnp.float32)
        half_east = 0.5 * east[height].astype(jnp.float32)
        half_north = 0.5 * north[height].astype(jnp.float32)
        is_east = height < open_to_east
        is_north = height < open_to_north
        minus = jnp.where(is_east, half_east - spread, 0.0)
        plus = jnp.where(is_east, half_east + spread, 0.0)
        east_minus[at(height), :] = minus
        east_plus[at(height), :] = plus
        north_minus[at(height), :] = jnp.where(is_north, half_north - spread, 0.0)
        north_plus[at(height), :] = jnp.where(is_north, half_north + spread, 0.0)
        return (
            pack(packs[0], own, height),
            pack(packs[1], minus, height),
            pack(packs[2], plus, height),
        )

    start_pack, minus_pack, plus_pack = loop(coefficients, (zero, zero, zero))
    minus_row = north_row(north_minus)
    plus_row = north_row(north_plus)
    to_east0[0] = plus_pack * start_pack
    to_east0[1] = minus_pack
    to_west0[...] = start_pack
    to_north0[0] = plus_row * north_row(start)
    to_north0[1] = minus_row
    to_south0[...] = south_row(start)

    first = {
        NORTH: remote(to_north0, from_south0, 0, NORTH),
        SOUTH: remote(to_south0, from_north0, 0, SOUTH),
        EAST: remote(to_east0, from_west0, 0, EAST),
        WEST: remote(to_west0, from_east0, 0, WEST),
    }
    exchanges = [first] + [
        {
            NORTH: remote(to_north.at[slot], from_south.at[slot], slot + 1, NORTH),
            SOUTH: remote(to_south.at[slot], from_north.at[slot], slot + 1, SOUTH),
            EAST: remote(to_east.at[slot], from_west.at[slot], slot + 1, EAST),
            WEST: remote(to_west.at[slot], from_east.at[slot], slot + 1, WEST),
        }
        for slot in range(3)
    ]

    def send(turn):
        for side in (NORTH, SOUTH, EAST, WEST):
            exchanges[turn][side].start()

    def receive(turn):
        for side in (EAST, WEST, NORTH, SOUTH):
            exchanges[turn][side].wait_recv()

    pl.semaphore_wait(barrier, 4)
    send(0)

    for load in loads[6:]:
        load.wait()
    wet = count[...]

    def factor(height, last):
        last_ratio, upper = last
        lower = jnp.where(
            height + 1 < wet, vertical[jnp.minimum(height, levels - 2)].astype(jnp.float32), 0.0
        )
        lower = jnp.where(height < levels - 1, lower, 0.0)
        inverted = 1.0 / (1.0 + upper + lower - upper * last_ratio)
        following = lower * inverted
        inverse[at(height), :] = inverted
        ratio[at(height), :] = following
        feed[at(height), :] = upper * inverted
        return following, lower

    loop(factor, (zero, zero), CHAIN_UNROLL)

    def step_inside(state):
        def body(height, nothing):
            own = state[at(height), :]
            plus_x, minus_x = east_plus[at(height), :], east_minus[at(height), :]
            plus_y, minus_y = north_plus[at(height), :], north_minus[at(height), :]
            flux_x = plus_x * own + minus_x * from_lane_east(own)
            flux_y = plus_y * own + minus_y * from_row_north(own)
            spread = (flux_x - from_lane_west(flux_x)) + (flux_y - from_row_south(flux_y))
            rate = sink[at(height), :]
            rhs[at(height), :] = own - spread - rate * jnp.tanh(own)
            return nothing

        loop(body, 0)

    def sink_rates(height, nothing):
        sink[at(height), :] = jnp.where(height < wet, relax[height].astype(jnp.float32), 0.0)
        return nothing

    loop(sink_rates, 0)
    step_inside(start)

    def eliminate(rim):
        def body(height, last):
            right = rhs[at(height), :] + unpack(rim, height)
            new = right * inverse[at(height), :] + feed[at(height), :] * last
            carry[at(height), :] = new
            return new

        loop(body, zero, CHAIN_UNROLL)

    def substitute(visit, init):
        def body(step, state):
            height = levels - 1 - step
            last, kept = state
            new = carry[at(height), :] + ratio[at(height), :] * last
            return new, visit(height, new, kept)

        return loop(body, (zero, init), CHAIN_UNROLL)[1]

    def solve_into(target):
        def visit(height, value, packed):
            target[at(height), :] = value
            return pack(packed, value, height)

        return substitute(visit, zero)

    def to_even(packed):
        return pltpu.roll(packed, 1, 1)

    def to_odd(packed):
        return pltpu.roll(packed, lanes - 1, 1)

    def step_rims(state, state_pack, west_product, east_state, south_product, north_state):
        add_rows(rhs, south_product + south_minus * south_row(state), -minus_row * north_state)
        return jnp.where(
            even_lane, to_even(west_product) + west_minus * state_pack, -minus_pack * to_odd(east_state)
        )

    receive(0)
    west_minus = to_even(from_west0[1])
    south_minus = from_south0[1]
    rim = step_rims(
        start, start_pack, from_west0[0], from_east0[...], from_south0[0], from_north0[...]
    )
    eliminate(rim)
    middle_pack = solve_into(middle)
    to_north[0] = plus_row * north_row(middle)
    to_south[0] = south_row(middle)
    to_east[0] = plus_pack * middle_pack
    to_west[0] = middle_pack
    send(1)
    step_inside(middle)
    receive(1)
    rim = step_rims(middle, middle_pack, from_west[0], from_east[0], from_south[0], from_north[0])
    eliminate(rim)

    def misfit(height, value, nothing):
        seen = observed[height].astype(jnp.float32)
        rhs[at(height), :] = jnp.where(height < wet, value - seen, 0.0)
        return nothing

    substitute(misfit, 0)
    eliminate(zero)
    two_pack = solve_into(solved_two)
    to_north[1] = north_row(solved_two)
    to_south[1] = south_row(solved_two)
    to_east[1] = two_pack
    to_west[1] = two_pack
    send(2)

    def adjoint_inside(solved, state, target, with_gradient):
        def body(height, nothing):
            own = solved[at(height), :]
            value = state[at(height), :]
            slope_x = from_lane_east(own) - own
            slope_y = from_row_north(own) - own
            squeeze = jnp.tanh(value)
            total = own * (1.0 - sink[at(height), :] * (1.0 - squeeze * squeeze))
            total = total + east_plus[at(height), :] * slope_x
            total = total + from_lane_west(east_minus[at(height), :] * slope_x)
            total = total + north_plus[at(height), :] * slope_y
            total = total + from_row_south(north_minus[at(height), :] * slope_y)
            target[at(height), :] = total
            if with_gradient:
                gradient_inside(height, slope_x, slope_y, value, True)
            return nothing

        loop(body, 0)

    def gradient_inside(height, slope_x, slope_y, value, more):
        rise_x = pltpu.roll(value, lanes - 1, 1) - value
        rise_y = pltpu.roll(value, rows - 1, 0) - value
        inner_x = (height < open_to_east) & (lane < lanes - 1)
        inner_y = (height < open_to_north) & (row < rows - 1)
        part = jnp.where(inner_x, slope_x * rise_x, 0.0) + jnp.where(inner_y, slope_y * rise_y, 0.0)
        if more:
            gradient[at(height), :] = gradient[at(height), :] - part
        else:
            gradient[at(height), :] = -part

    lane_level = ((lane + 1) % lanes) // 2
    odd_open = (lane_level < open_to_east[:, lanes - 1 :]) & (lane % 2 == 1)
    row_level = lax.broadcasted_iota(jnp.int32, (levels, lanes), 0)
    row_open = row_level < open_to_north[rows - 1 :, :]

    def gradient_rims(solved, solved_pack, state, state_pack, solved_east, state_east, solved_north, state_north):
        packed = (to_odd(solved_east) - solved_pack) * (to_odd(state_east) - state_pack)
        lined = (solved_north - north_row(solved)) * (state_north - north_row(state))
        return jnp.where(odd_open, -packed, 0.0), jnp.where(row_open, -lined, 0.0)

    def adjoint_rims(solved, solved_pack, turn, target):
        add_rows(
            target,
            south_minus * (south_row(solved) - from_south[turn]),
            plus_row * from_north[turn],
        )
        return jnp.where(
            even_lane,
            west_minus * (solved_pack - to_even(from_west[turn])),
            plus_pack * to_odd(from_east[turn]),
        )

    adjoint_inside(solved_two, middle, rhs, False)
    receive(2)
    rim = adjoint_rims(solved_two, two_pack, 1, rhs)
    eliminate(rim)
    one_pack = solve_into(solved_one)
    to_north[2] = north_row(solved_one)
    to_south[2] = south_row(solved_one)
    to_east[2] = one_pack
    to_west[2] = one_pack
    send(3)

    late_rim, late_row = gradient_rims(
        solved_two, two_pack, middle, middle_pack,
        from_east[1], from_east[0], from_north[1], from_north[0],
    )

    def late_gradient(height, nothing):
        own = solved_two[at(height), :]
        slope_x = pltpu.roll(own, lanes - 1, 1) - own
        slope_y = pltpu.roll(own, rows - 1, 0) - own
        gradient_inside(height, slope_x, slope_y, middle[at(height), :], False)
        return nothing

    loop(late_gradient, 0)
    adjoint_inside(solved_one, start, rhs, True)
    receive(3)
    rim = adjoint_rims(solved_one, one_pack, 2, rhs)
    early_rim, early_row = gradient_rims(
        solved_one, one_pack, start, start_pack,
        from_east[2], from_east0[...], from_north[2], from_north0[...],
    )
    add_rows(gradient, jnp.zeros_like(early_row), late_row + early_row)
    gradient_rim = late_rim + early_rim

    def finish(height, nothing):
        rhs[at(height), :] = rhs[at(height), :] + unpack(rim, height)
        gradient[at(height), :] = gradient[at(height), :] + unpack(gradient_rim, height)
        return nothing

    loop(finish, 0)
    stores = [
        pltpu.make_async_copy(rhs, adjoint_hbm, store_sem.at[0]),
        pltpu.make_async_copy(gradient, gradient_hbm, store_sem.at[1]),
    ]
    for store in stores:
        store.start()
    for exchange in exchanges:
        for side in range(4):
            exchange[side].wait_send()
    for store in stores:
        store.wait()


def per_device(sizes, tracer_start, *others):
    levels, rows, lanes, _, _ = sizes
    flat = (levels * rows, lanes)
    field = pltpu.VMEM(flat, jnp.float32)
    columns = pltpu.VMEM((rows, lanes), jnp.float32)
    lines = pltpu.VMEM((levels, lanes), jnp.float32)

    def several(count, shape):
        return pltpu.VMEM((count,) + shape, jnp.float32)

    column, line = (rows, lanes), (levels, lanes)
    scratch = [field]
    scratch += [pltpu.VMEM(other.shape, other.dtype) for other in others]
    scratch += [field] * 14
    scratch += [several(2, column), several(2, line), columns, lines]
    scratch += [several(3, column), several(3, column), several(3, line), several(3, line)]
    scratch += [several(2, column), several(2, line), columns, lines]
    scratch += [several(3, column), several(3, column), several(3, line), several(3, line)]
    scratch += [
        pltpu.SemaphoreType.DMA((10,)),
        pltpu.SemaphoreType.DMA((2,)),
        pltpu.SemaphoreType.DMA((4, 4)),
        pltpu.SemaphoreType.DMA((4, 4)),
    ]
    out = jax.ShapeDtypeStruct(flat, jnp.float32)
    adjoint, gradient = pl.pallas_call(
        functools.partial(kernel, sizes),
        out_shape=(out, out),
        in_specs=[pl.BlockSpec(memory_space=pl.ANY)] * 10,
        out_specs=(pl.BlockSpec(memory_space=pl.ANY),) * 2,
        scratch_shapes=scratch,
        compiler_params=pltpu.CompilerParams(collective_id=0, has_side_effects=True),
    )(tracer_start.reshape(flat), *others)
    return adjoint.reshape(tracer_start.shape), gradient.reshape(tracer_start.shape)


def solution(mesh):
    block = P(None, "ty", "tx")
    plane = P("ty", "tx")
    size_y, size_x = mesh.shape["ty"], mesh.shape["tx"]

    def program(tracer_start, *others):
        levels, all_rows, all_lanes = tracer_start.shape
        sizes = (levels, all_rows // size_y, all_lanes // size_x, size_y, size_x)
        return jax.shard_map(
            functools.partial(per_device, sizes),
            mesh=mesh,
            in_specs=(block,) * 7 + (plane,) * 3,
            out_specs=(block, block),
            check_vma=False,
        )(tracer_start, *others)

    return program
```

profile of v0, /device:TPU:2, one launch (start us, length us, event | category | flops | bytes accessed | tf_op | source)
XLA Modules:
  0.0 43.0 jit_solution(3212473956837868731)
XLA Ops:
  0.6 39.7 %shard_map.113 = (f32[768,128]{1,0:T(8,128)}, f32[768,128]{1,0:T(8,128)}) custom-call(f32[768,128]{1,0:T(8,128)} %bitcast.5, bf16[48,16,128]{2,1,0:T(8,128)(2,1)} %observed_hbm.1, bf16[48,16,128]{2,1,0:T(8,128)(2,1)} %east_hbm.1, bf16[48,16,128]{2,1,0:T(8,128)(2,1)} %north_hbm.1, bf16[48,16,128]{2,1,0:T(8,128)(2,1)} %mixing_hbm.1, ...), custom_call_target="tpu_custom_call" | custom-call | tf_op jit(solution)/shard_map/pallas_call | solution.py:421
  40.4 0.0 copy-start
  40.4 1.8 %copy.14 = f32[48,16,128]{2,1,0:T(8,128)} copy(f32[48,16,128]{2,1,0:T(8,128)} %bitcast.4) | data formatting | bytes 786432
  42.2 0.0 copy-done
  42.2 0.7 %copy.15 = f32[48,16,128]{2,1,0:T(8,128)} copy(f32[48,16,128]{2,1,0:T(8,128)S(1)} %bitcast.3) | data formatting | bytes 786432
Async XLA Ops:
  40.4 1.8 %copy-start = (f32[768,128]{1,0:T(8,128)S(1)}, f32[768,128]{1,0:T(8,128)}, u32[]{:S(2)}) copy-start(f32[768,128]{1,0:T(8,128)} %get-tuple-element.5) | copy-start | bytes 1179652
where the time goes:
time: 43.1 us; the launch traced here: 43 us
  Pallas kernels  39.7 us (92%)
  local copies, waits for them, and re-layouts  2.57 us (6%)
  between operations  0.65 us (2%)
    pallas_call x1, Pallas kernels, per_device(): pl.pallas_call(functools.partial(kernel, sizes), out_shape=(out, out), in...  39.7 us
    unnamed x4, local copies, waits for them, and re-layouts  2.57 us

commit v1 on v0

--- a/solution.py
+++ b/solution.py
@@ -8,24 +8,26 @@
 from jax.sharding import PartitionSpec as P
 
 EAST, WEST, NORTH, SOUTH = range(4)
-UNROLL = 4
-CHAIN_UNROLL = 8
+UNROLL = 16
+CHAIN_UNROLL = 48
+PIECES = 4
+VMEM_LIMIT = 16 * 1024 * 1024
 
 
 def kernel(
     sizes,
     tracer_hbm, observed_hbm, east_hbm, north_hbm, mixing_hbm, vertical_hbm, relax_hbm,
     count_hbm, face_east_hbm, face_north_hbm,
-    adjoint_hbm, gradient_hbm,
+    inside, gradient, result_rims,
     start, observed, east, north, mixing, vertical, relax, count, face_east, face_north,
     east_minus, east_plus, north_minus, north_plus, sink,
     inverse, ratio, feed,
-    middle, rhs, carry, solved_two, solved_one, gradient,
+    middle, rhs, carry, solved_two, solved_one,
     to_east0, to_north0, to_west0, to_south0,
     to_east, to_west, to_north, to_south,
     from_west0, from_south0, from_east0, from_north0,
     from_west, from_east, from_south, from_north,
-    load_sem, store_sem, send_sem, recv_sem,
+    load_sem, send_sem, recv_sem,
 ):
     levels, rows, lanes, size_y, size_x = sizes
     my_y = lax.axis_index("ty")
@@ -364,31 +366,39 @@
         return nothing
 
     loop(late_gradient, 0)
-    adjoint_inside(solved_one, start, rhs, True)
+    adjoint_inside(solved_one, start, inside, True)
     receive(3)
-    rim = adjoint_rims(solved_one, one_pack, 2, rhs)
+    result_rims[0] = adjoint_rims(solved_one, one_pack, 2, inside)
     early_rim, early_row = gradient_rims(
         solved_one, one_pack, start, start_pack,
         from_east[2], from_east0[...], from_north[2], from_north0[...],
     )
     add_rows(gradient, jnp.zeros_like(early_row), late_row + early_row)
-    gradient_rim = late_rim + early_rim
-
-    def finish(height, nothing):
-        rhs[at(height), :] = rhs[at(height), :] + unpack(rim, height)
-        gradient[at(height), :] = gradient[at(height), :] + unpack(gradient_rim, height)
-        return nothing
-
-    loop(finish, 0)
-    stores = [
-        pltpu.make_async_copy(rhs, adjoint_hbm, store_sem.at[0]),
-        pltpu.make_async_copy(gradient, gradient_hbm, store_sem.at[1]),
-    ]
-    for store in stores:
-        store.start()
+    result_rims[1] = late_rim + early_rim
     for exchange in exchanges:
         for side in range(4):
             exchange[side].wait_send()
+
+
+def finish(sizes, inside, gradient_inside, rims, adjoint_hbm, gradient_hbm, adjoint, gradient, store_sem):
+    levels, rows, lanes, _, _ = sizes
+    lane = lax.broadcasted_iota(jnp.int32, (rows, lanes), 1)
+    rim_lanes = (lane == 0) | (lane == lanes - 1)
+    stores = []
+    for piece in range(PIECES):
+        first, last = piece * levels // PIECES, (piece + 1) * levels // PIECES
+        for height in range(first, last):
+            here = slice(height * rows, (height + 1) * rows)
+            for slot, (source, target) in enumerate(((inside, adjoint), (gradient_inside, gradient))):
+                rim = pltpu.roll(rims[slot], (lanes - 2 * height) % lanes, 1)
+                target[here, :] = source[here, :] + jnp.where(rim_lanes, rim, 0.0)
+        part = slice(first * rows, last * rows)
+        for slot, (source, target) in enumerate(((adjoint, adjoint_hbm), (gradient, gradient_hbm))):
+            store = pltpu.make_async_copy(
+                source.at[part, :], target.at[part, :], store_sem.at[piece, slot]
+            )
+            store.start()
+            stores.append(store)
     for store in stores:
         store.wait()
 
@@ -406,26 +416,35 @@
     column, line = (rows, lanes), (levels, lanes)
     scratch = [field]
     scratch += [pltpu.VMEM(other.shape, other.dtype) for other in others]
-    scratch += [field] * 14
+    scratch += [field] * 13
     scratch += [several(2, column), several(2, line), columns, lines]
     scratch += [several(3, column), several(3, column), several(3, line), several(3, line)]
     scratch += [several(2, column), several(2, line), columns, lines]
     scratch += [several(3, column), several(3, column), several(3, line), several(3, line)]
     scratch += [
         pltpu.SemaphoreType.DMA((10,)),
-        pltpu.SemaphoreType.DMA((2,)),
         pltpu.SemaphoreType.DMA((4, 4)),
         pltpu.SemaphoreType.DMA((4, 4)),
     ]
     out = jax.ShapeDtypeStruct(flat, jnp.float32)
+    in_vmem = pl.BlockSpec(memory_space=pltpu.VMEM)
+    in_hbm = pl.BlockSpec(memory_space=pl.ANY)
+    parts = pl.pallas_call(
+        functools.partial(kernel, sizes),
+        out_shape=(out, out, jax.ShapeDtypeStruct((2,) + column, jnp.float32)),
+        in_specs=[in_hbm] * 10,
+        out_specs=(in_vmem,) * 3,
+        scratch_shapes=scratch,
+        compiler_params=pltpu.CompilerParams(collective_id=0, has_side_effects=True, vmem_limit_bytes=VMEM_LIMIT),
+    )(*[pltpu.with_memory_space_constraint(a, pltpu.HBM) for a in (tracer_start.reshape(flat), *others)])
     adjoint, gradient = pl.pallas_call(
-        functools.partial(kernel, sizes),
+        functools.partial(finish, sizes),
         out_shape=(out, out),
-        in_specs=[pl.BlockSpec(memory_space=pl.ANY)] * 10,
-        out_specs=(pl.BlockSpec(memory_space=pl.ANY),) * 2,
-        scratch_shapes=scratch,
-        compiler_params=pltpu.CompilerParams(collective_id=0, has_side_effects=True),
-    )(tracer_start.reshape(flat), *others)
+        in_specs=[in_vmem] * 3,
+        out_specs=(in_hbm,) * 2,
+        scratch_shapes=[field, field, pltpu.SemaphoreType.DMA((PIECES, 2))],
+        compiler_params=pltpu.CompilerParams(vmem_limit_bytes=VMEM_LIMIT),
+    )(*parts)
     return adjoint.reshape(tracer_start.shape), gradient.reshape(tracer_start.shape)
 
 

time: 43.1 us -> 37 us (0.86)
  Pallas kernels: 39.7 us -> 36.2 us
  local copies, waits for them, and re-layouts: 2.57 us -> 0 us
    pallas_call x1 -> x2, Pallas kernels: 39.7 us -> 36.2 us  [the longest x1 35.2 us: per_device(): pl.pallas_call(functools.partial(kernel, sizes), out_shape=(out, out, jax...]
    unnamed x4 -> x0, local copies, waits for them, and re-layouts: 2.57 us -> none
where the time goes in v1:
time: 37 us; the launch traced here: 36.8 us
  Pallas kernels  36.2 us (98%)
  between operations  0.64 us (2%)
    pallas_call x1, Pallas kernels, per_device(): pl.pallas_call(functools.partial(kernel, sizes), out_shape=(out, out, jax...  35.2 us
    pallas_call x1, Pallas kernels, per_device(): pl.pallas_call(functools.partial(finish, sizes), out_shape=(out, out), in...  1.05 us

profile of v1, /device:TPU:2, one launch (start us, length us, event | category | flops | bytes accessed | tf_op | source)
XLA Modules:
  0.0 36.8 jit_solution(12784861200524728188)
XLA Ops:
  0.6 35.2 %shard_map.113 = (f32[768,128]{1,0:T(8,128)S(1)}, f32[768,128]{1,0:T(8,128)S(1)}, f32[2,16,128]{2,1,0:T(8,128)S(1)}) custom-call(f32[768,128]{1,0:T(8,128)} %bitcast.3, bf16[48,16,128]{2,1,0:T(8,128)(2,1)} %observed_hbm.1, bf16[48,16,128]{2,1,0:T(8,128)(2,1)} %east_hbm.1, bf16[48,16,128]{2,1,0:T(8,128)(2,1)} %north_hbm.1, bf16[48,16,128]{2,1,0:T(8,128)(2,1)} %mixing_hbm.1, ...), custom_call_target="tpu_custom_call" | custom-call | tf_op jit(solution)/shard_map/pallas_call | solution.py:432
  35.8 1.0 %shard_map.114 = (f32[768,128]{1,0:T(8,128)}, f32[768,128]{1,0:T(8,128)}) custom-call(f32[768,128]{1,0:T(8,128)S(1)} %get-tuple-element.7.inside, f32[768,128]{1,0:T(8,128)S(1)} %get-tuple-element.8.gradient_inside, f32[2,16,128]{2,1,0:T(8,128)S(1)} %get-tuple-element.9.rims), custom_call_target="tpu_custom_call" | custom-call | tf_op jit(solution)/shard_map/pallas_call | solution.py:440
